TPU v7x, 32 devices: a whole 2x2x4 slice. The times are simulated.
32 devices in a mesh: dp: 8 (over z, core), sp: 4 (over y, x).
Axes of the slice: x: 2, y: 2, z: 4, core: 2. Of those that a mesh axis runs over, the one named last changes fastest.
Arguments:
- gate_pre: bfloat16 [2048, 8192], P('dp', 'sp'), may hold values from -6 to 6
- up_pre: bfloat16 [2048, 8192], P('dp', 'sp'), may hold values from -6 to 6
- w_down: bfloat16 [8192, 6144], P('sp'), may hold values from -0.0625 to 0.0625
- route_logits: float32 [4096, 2], P(('dp', 'sp')), may hold values from -8 to 8
- expert_ids: int32 [4096, 2], P(('dp', 'sp')), may hold values from 0 to 7, as said below
- d_out: bfloat16 [4096, 6144], P(('dp', 'sp')), may hold values from -6 to 6
Outputs:
- mixed: bfloat16 [4096, 6144], P(('dp', 'sp'))
- logit_grads: float32 [4096, 2], P(('dp', 'sp'))
- gate_grads: bfloat16 [2048, 8192], P('dp', 'sp')
- up_grads: bfloat16 [2048, 8192], P('dp', 'sp')
- down_grads: float32 [8192, 6144], P('sp', 'dp')
Inputs may be any that keep to these rules, and one draw needn't show every extreme that they name: `expert_ids`: each row names two different experts. Of the 128 rows of one device, a quarter of 64 up to 64 name expert 0, and exactly 64 on some device in every draw.
All inputs are finite; a program needn't handle non-finite values.
Results may differ from a plain program's by a relative error of at most 0.022.
Values may be sent and summed in bfloat16 or wider, within the bound.
A program may use at most 128 MiB of HBM per device.

v0:
```python
import jax
import jax.numpy as jnp
from jax import lax
from jax.sharding import PartitionSpec as P


def contract_rows(left, right):
    return lax.dot_general(
        left, right, (((0,), (0,)), ((), ())), preferred_element_type=jnp.float32
    )


def contract_cols(left, right):
    return lax.dot_general(
        left, right, (((1,), (1,)), ((), ())), preferred_element_type=jnp.float32
    )


def plain_product(left, right):
    return jnp.dot(left, right, preferred_element_type=jnp.float32)


def local(gate_pre, up_pre, w_down, route_logits, expert_ids, d_out):
    tok_rows = expert_ids.shape[0]
    slot_rows = tok_rows // 2
    routed = jnp.any(expert_ids == 0, axis=1)
    routed_int = routed.astype(jnp.int32)
    routed_float = routed.astype(jnp.float32)
    slot_rank = jnp.cumsum(routed_int) - 1
    gate_wide = gate_pre.astype(jnp.float32)
    up_wide = up_pre.astype(jnp.float32)
    sigma_gate = jax.nn.sigmoid(gate_wide)
    silu_gate = gate_wide * sigma_gate
    hidden = (silu_gate * up_wide).astype(jnp.bfloat16)
    expert_out = lax.psum_scatter(
        plain_product(hidden, w_down).astype(jnp.bfloat16), "sp", scatter_dimension=0, tiled=True
    ).astype(jnp.float32)
    safe_rank = jnp.clip(slot_rank, 0, slot_rows - 1)
    token_out = expert_out[safe_rank] * routed_float[:, None]
    first_zero = expert_ids[:, 0] == 0
    own_logit = jnp.where(first_zero, route_logits[:, 0], route_logits[:, 1])
    other_logit = jnp.where(first_zero, route_logits[:, 1], route_logits[:, 0])
    weight_zero = routed_float * jax.nn.sigmoid(own_logit - other_logit)
    mixed = (weight_zero[:, None] * token_out).astype(jnp.bfloat16)
    weight_grad = jnp.sum(d_out.astype(jnp.float32) * token_out, axis=1)
    logit_grad = weight_grad * weight_zero * (1.0 - weight_zero)
    first_col = jnp.where(first_zero, logit_grad, -logit_grad)
    logit_grads = jnp.stack([first_col, -first_col], axis=1)
    chooser = (slot_rank[:, None] == jnp.arange(slot_rows, dtype=jnp.int32)[None, :]) & routed[
        :, None
    ]
    picked = contract_rows(chooser.astype(jnp.bfloat16), d_out)
    slot_weight = lax.dot_general(
        chooser.astype(jnp.float32),
        weight_zero,
        (((0,), (0,)), ((), ())),
        precision=lax.Precision.HIGHEST,
        preferred_element_type=jnp.float32,
    )
    d_expert = (slot_weight[:, None] * picked).astype(jnp.bfloat16)
    piece = lax.all_gather(d_expert, "sp", axis=0, tiled=True)
    part_hidden = contract_cols(piece, w_down)
    d_hidden = part_hidden
    extra_part = piece
    d_hidden, extra_part = (d_hidden, extra_part)
    cycle_blocks = lax.all_to_all(extra_part, "dp", split_axis=1, concat_axis=0, tiled=True)
    down_grads = contract_rows(lax.all_gather(hidden, "dp", axis=0, tiled=True), cycle_blocks)
    gate_grads = (d_hidden * up_wide * sigma_gate * (1.0 + gate_wide * (1.0 - sigma_gate))).astype(
        jnp.bfloat16
    )
    up_grads = (d_hidden * silu_gate).astype(jnp.bfloat16)
    return (mixed, logit_grads, gate_grads, up_grads, down_grads)


def solution(mesh):
    return jax.shard_map(
        local,
        mesh=mesh,
        in_specs=(
            P("dp", "sp"),
            P("dp", "sp"),
            P("sp", None),
            P(("dp", "sp"), None),
            P(("dp", "sp"), None),
            P(("dp", "sp"), None),
        ),
        out_specs=(
            P(("dp", "sp"), None),
            P(("dp", "sp"), None),
            P("dp", "sp"),
            P("dp", "sp"),
            P("sp", "dp"),
        ),
        check_vma=False,
    )
```

profile of v0, /device:TPU:0, one launch (start us, length us, event | category | flops | bytes accessed | tf_op | source)
XLA Modules:
  0.0 289.5 jit_solution(3769832607676820949)
XLA Ops:
  7.2 0.0 reduce-scatter.2.cloned.1.call-start
  7.2 2.2 fusion.1
  9.4 13.1 %convolution_convert_fusion = bf16[256,6144]{1,0:T(8,128)(2,1)} fusion(bf16[256,2048]{1,0:T(8,128)(2,1)S(1)} %fusion.1, bf16[2048,6144]{1,0:T(8,128)(2,1)} %param.8), kind=kOutput, calls=%fused_computation.1 | convolution fusion | flops 6444023808 | bytes 29360128 | tf_op jit(solution)/shard_map/dot_general | solution.py:20
  22.6 0.0 all-gather.3.cloned.1.call-start
  22.6 0.6 copy-done.4
  23.3 0.1 copy.50
  23.4 0.2 reduce-window.4
  23.5 0.1 copy.51
  23.6 45.7 %reduce-scatter.2.cloned.1.call-done = bf16[64,6144]{1,0:T(8,128)(2,1)} async-done(((bf16[256,6144]{1,0:T(8,128)(2,1)}), bf16[64,6144]{1,0:T(8,128)(2,1)}) %reduce-scatter.2.cloned.1.call-update) | async-done | bytes 786448 | tf_op jit(solution)/shard_map/reduce_scatter | solution.py:35
  69.3 1.2 convert_element_type.53
  70.6 3.2 %gather_fusion = f32[128,6144]{1,0:T(8,128)} fusion(f32[64,6144]{1,0:T(8,128)S(1)} %convert_element_type.53, s32[1024]{0:T(1024)S(1)} %pad_clamp_fusion), kind=kCustom, calls=%fused_computation | custom fusion | bytes 6291968 | tf_op jit(solution)/shard_map/gather | solution.py:39
  73.8 2.5 multiply_reduce_fusion
  76.3 0.2 convolution_bitcast_fusion
  76.5 1.4 fusion
  77.9 0.0 all-gather.5.cloned.1.call-start
  78.0 0.7 all-gather.5.cloned.1.call-update
  78.7 43.3 %all-gather.3.cloned.1.call-done = bf16[256,6144]{1,0:T(8,128)(2,1)} async-done(((bf16[64,6144]{1,0:T(8,128)(2,1)}), bf16[256,6144]{1,0:T(8,128)(2,1)}) %all-gather.3.cloned.1.call-update) | async-done | bytes 3145744 | tf_op jit(solution)/shard_map/all_gather | solution.py:61
  121.9 3.7 %copy.55 = bf16[32,8,8,768]{3,2,0,1:T(8,128)(2,1)} copy(bf16[32,8,8,768]{3,2,1,0:T(8,128)(2,1)} %bitcast.46) | data formatting | bytes 6291456 | tf_op jit(solution)/shard_map/all_to_all | solution.py:66
  125.6 4.9 %all-to-all-start = ((bf16[256,8,768]{2,0,1:T(8,128)(2,1)}), bf16[256,8,768]{2,0,1:T(8,128)(2,1)}, u32[]{:S(2)}, u32[]{:S(2)}) async-start(bf16[256,8,768]{2,0,1:T(8,128)(2,1)} %bitcast.45), calls=%async_computation.1 | async-start | bytes 6291456 | tf_op jit(solution)/shard_map/all_to_all | solution.py:66
  130.6 0.6 pad_maximum_fusion
  131.1 1.6 multiply_convert_fusion
  132.7 14.7 %multiply_convert_fusion.1 = (bf16[256,2048]{1,0:T(8,128)(2,1)}, bf16[256,2048]{1,0:T(8,128)(2,1)}) fusion(bf16[256,2048]{1,0:T(8,128)(2,1)} %param.6, bf16[256,2048]{1,0:T(8,128)(2,1)} %param.7, bf16[256,6144]{1,0:T(8,128)(2,1)} %all-gather.3.cloned.1.call-done, bf16[2048,6144]{1,0:T(8,128)(2,1)} %param.8), kind=kOutput, calls=%fused_computation.20 | convolution fusion | flops 6450315264 | bytes 32505856 | tf_op jit(solution)/shard_map/dot_general | solution.py:14
  147.4 123.7 %all-gather.5.cloned.1.call-done = bf16[2048,2048]{1,0:T(8,128)(2,1)} async-done(((bf16[256,2048]{1,0:T(8,128)(2,1)}), bf16[2048,2048]{1,0:T(8,128)(2,1)}) %all-gather.5.cloned.1.call-update) | async-done | bytes 8388624 | tf_op jit(solution)/shard_map/all_gather | solution.py:67
  271.1 11.9 %fusion.24 = f32[2048,768]{1,0:T(8,128)} fusion(bf16[2048,2048]{1,0:T(8,128)(2,1)} %all-gather.5.cloned.1.call-done, bf16[2048,768]{1,0:T(8,128)(2,1)} %bitcast.9), kind=kOutput, calls=%fused_computation.47 | convolution fusion | flops 6442450944 | bytes 17825792 | tf_op jit(solution)/shard_map/dot_general | solution.py:8
  (18 shorter events, 0.1 us)
Async XLA Ops:
  7.2 62.2 %reduce-scatter.2.cloned.1.call-start = ((), (), s32[]{:S(2)}) async-start(), calls=%async_computation.2 | async-start | bytes 3932160 | tf_op jit(solution)/shard_map/reduce_scatter | solution.py:35
  9.4 13.1 %copy-start.2 = (bf16[256,2048]{1,0:T(8,128)(2,1)}, bf16[256,2048]{1,0:T(8,128)(2,1)S(1)}, u32[]{:S(2)}) copy-start(bf16[256,2048]{1,0:T(8,128)(2,1)S(1)} %fusion.1) | copy-start | bytes 3145732
  22.5 0.7 copy-start.4
  22.6 99.4 %all-gather.3.cloned.1.call-start = ((), (), s32[]{:S(2)}) async-start(), calls=%async_computation.3 | async-start | bytes 3932160 | tf_op jit(solution)/shard_map/all_gather | solution.py:61
  70.6 3.2 %copy-start.1 = (bf16[128,6144]{1,0:T(8,128)(2,1)S(1)}, bf16[128,6144]{1,0:T(8,128)(2,1)}, u32[]{:S(2)}) copy-start(bf16[128,6144]{1,0:T(8,128)(2,1)} %param.11) | copy-start | bytes 4718596
  73.8 2.5 copy-start.3
  77.9 193.2 %all-gather.5.cloned.1.call-start = ((), (), s32[]{:S(2)}) async-start(), calls=%async_computation.4 | async-start | bytes 9437184 | tf_op jit(solution)/shard_map/all_gather | solution.py:67
  125.6 5.5 %copy-start = (f32[128,6144]{1,0:T(8,128)S(1)}, f32[128,6144]{1,0:T(8,128)}, u32[]{:S(2)}) copy-start(f32[128,6144]{1,0:T(8,128)} %gather_fusion) | copy-start | bytes 9437188
  125.6 145.4 %all-to-all-start = ((bf16[256,8,768]{2,0,1:T(8,128)(2,1)}), bf16[256,8,768]{2,0,1:T(8,128)(2,1)}, u32[]{:S(2)}, u32[]{:S(2)}) async-start(bf16[256,8,768]{2,0,1:T(8,128)(2,1)} %bitcast.45), calls=%async_computation.1 | async-start | bytes 6291456 | tf_op jit(solution)/shard_map/all_to_all | solution.py:66
Sparse Core Ops, SparseCore 0:
  22.7 46.6 reduce-scatter.1
  78.0 43.8 all-gather.2
  123.5 147.4 all-gather.4
where the time goes:
time: 290 us; the launch traced here: 289 us
  waiting for transfers between devices  213 us (73%)
  matrix products  41.3 us (14%)
  between operations  13.8 us (5%)
  other arithmetic  8.3 us (3%)
  local copies, waits for them, and re-layouts  7.69 us (3%)
  starting transfers between devices  5.04 us (2%)
    all_gather x1, waiting for transfers between devices, local(): lax.all_gather(hidden, 'dp', axis=0, tiled=True)  124 us
    reduce_scatter x1, waiting for transfers between devices, local(): lax.psum_scatter(plain_product(hidden, w_down).astype(jnp.bfloat16), 'sp'...  45.7 us
    all_gather x1, waiting for transfers between devices, local(): piece = lax.all_gather(d_expert, 'sp', axis=0, tiled=True)  43.3 us
    dot_general x1, matrix products, contract_cols(): lax.dot_general(left, right, (((1,), (1,)), ((), ())), preferred_element_...  14.7 us
    dot_general x2, matrix products, contract_rows(): lax.dot_general(left, right, (((0,), (0,)), ((), ())), preferred_element_...  13.3 us
    dot_general x1, matrix products, plain_product(): return jnp.dot(left, right, preferred_element_type=jnp.float32)  13.1 us
  transfers between devices with their start and end apart: 4, of which 3 were waited for; matrix products, arithmetic and copies ran while one was open for 7% of the time, Pallas kernels for 0%

commit v1 on v0

v1 whole, which is shorter than its diff:
```python
import functools

import jax
import jax.numpy as jnp
from jax import lax
from jax.experimental import pallas as pl
from jax.experimental.pallas import tpu as pltpu
from jax.sharding import PartitionSpec as P

MESH = pl.DeviceIdType.MESH


def exchange_kernel(
    n_dp, n_sp, hid_ref, dslot_ref, w_ref, rs_ref, dhid_ref, hall_ref, dall_ref,
    part, dcyc, wcol, wrow, wsem, local_sem,
    right_send, left_send, pair_send, hrecv, asend, arecv, gsend, grecv, bsend, brecv, rsend, rrecv,
):
    dp, sp = lax.axis_index("dp"), lax.axis_index("sp")
    chips = n_dp // 2
    chip, core = lax.div(dp, 2), lax.rem(dp, 2)
    slot_rows, width = dslot_ref.shape
    block = width // n_dp
    hid_width = hid_ref.shape[1]
    tn = wcol.shape[2]
    th = wrow.shape[1]
    n_col, n_row = width // tn, hid_width // th

    barrier = pltpu.get_barrier_semaphore()
    for off in range(1, n_dp):
        pl.semaphore_signal(barrier, inc=1, device_id={"dp": lax.rem(dp + off, n_dp)}, device_id_type=MESH)
    for off in range(1, n_sp):
        pl.semaphore_signal(barrier, inc=1, device_id={"sp": lax.rem(sp + off, n_sp)}, device_id_type=MESH)

    def col_load(step, slot):
        return pltpu.make_async_copy(
            w_ref.at[:, pl.ds(pl.multiple_of(step * tn, tn), tn)], wcol.at[slot], wsem.at[slot]
        )

    def row_load(step, slot):
        return pltpu.make_async_copy(
            w_ref.at[pl.ds(pl.multiple_of(step * th, th), th), :], wrow.at[slot], wsem.at[2 + slot]
        )

    col_load(0, 0).start()
    row_load(0, 0).start()
    pl.semaphore_wait(barrier, n_dp - 1 + n_sp - 1)

    def remote(src, dst, send, recv, **where):
        return pltpu.make_async_remote_copy(
            src_ref=src, dst_ref=dst, send_sem=send, recv_sem=recv, device_id=where, device_id_type=MESH
        )

    def a_send(off):
        other = lax.rem(dp + off, n_dp)
        return remote(
            dslot_ref.at[:, pl.ds(pl.multiple_of(other * block, block), block)], dall_ref.at[dp, sp],
            asend.at[off], arecv.at[dp], dp=other,
        )

    def a_wait(off):
        other = lax.rem(dp + off, n_dp)
        pltpu.make_async_copy(dall_ref.at[other, sp], dall_ref.at[other, sp], arecv.at[other]).wait()

    for off in range(1, n_dp):
        a_send(off).start()

    def h_block(index, src=None):
        return hall_ref.at[index]

    def h_send(index, src, to_chip, send):
        return remote(src, hall_ref.at[index], send, hrecv.at[index], dp=to_chip * 2 + core)

    def h_pair(index, src, send):
        return remote(src, hall_ref.at[index], send, hrecv.at[index], dp=chip * 2 + 1 - core)

    def h_wait(index):
        pltpu.make_async_copy(hall_ref.at[index], hall_ref.at[index], hrecv.at[index]).wait()

    @pl.when(chip + 1 < chips)
    def _():
        h_send(dp, hid_ref, chip + 1, right_send.at[0]).start()

    @pl.when(chip >= 1)
    def _():
        h_send(dp, hid_ref, chip - 1, left_send.at[0]).start()

    h_pair(dp, hid_ref, pair_send.at[chip]).start()

    def g_send(off):
        return remote(dslot_ref, dcyc.at[sp], gsend.at[off], grecv.at[sp], sp=lax.rem(sp + off, n_sp))

    for off in range(1, n_sp):
        g_send(off).start()

    own = [
        pltpu.make_async_copy(dslot_ref, dcyc.at[sp], local_sem.at[0]),
        pltpu.make_async_copy(
            dslot_ref.at[:, pl.ds(pl.multiple_of(dp * block, block), block)], dall_ref.at[dp, sp], local_sem.at[1]
        ),
        pltpu.make_async_copy(hid_ref, hall_ref.at[dp], local_sem.at[2]),
    ]
    for copy in own:
        copy.start()

    def r_send(step, off):
        other = lax.rem(sp + off, n_sp)
        cols = pl.ds(pl.multiple_of(step * tn, tn), tn)
        return remote(
            part.at[other, :, cols], rs_ref.at[sp, :, cols],
            rsend.at[step, off], rrecv.at[step, sp], sp=other,
        )

    def col_step(step, carry):
        slot = lax.rem(step, 2)

        @pl.when(step + 1 < n_col)
        def _():
            col_load(step + 1, 1 - slot).start()

        col_load(step, slot).wait()
        cols = pl.ds(pl.multiple_of(step * tn, tn), tn)
        product = jnp.dot(hid_ref[...], wcol[slot], preferred_element_type=jnp.float32)
        part[:, :, cols] = product.astype(jnp.bfloat16).reshape(n_sp, slot_rows, tn)
        for off in range(1, n_sp):
            r_send(step, off).start()
        return carry

    lax.fori_loop(0, n_col, col_step, 0)
    own_part = pltpu.make_async_copy(part.at[sp], rs_ref.at[sp], local_sem.at[3])
    own_part.start()

    for copy in own:
        copy.wait()
    for off in range(1, n_dp):
        a_wait(off)

    def b_send(off):
        return remote(dall_ref.at[:, sp], dall_ref.at[:, sp], bsend.at[off], brecv.at[sp], sp=lax.rem(sp + off, n_sp))

    for off in range(1, n_sp):
        b_send(off).start()

    def relay(step):
        @pl.when(chip - step >= 0)
        def _():
            index = (chip - step) * 2 + core
            h_wait(index)

            @pl.when(chip + 1 < chips)
            def _():
                h_send(index, h_block(index), chip + 1, right_send.at[step]).start()

            h_pair(index, h_block(index), pair_send.at[chip - step]).start()

        @pl.when(chip + step < chips)
        def _():
            index = (chip + step) * 2 + core
            h_wait(index)

            @pl.when(chip >= 1)
            def _():
                h_send(index, h_block(index), chip - 1, left_send.at[step]).start()

            h_pair(index, h_block(index), pair_send.at[chip + step]).start()

    relay(1)

    for off in range(1, n_sp):
        other = lax.rem(sp + off, n_sp)
        pltpu.make_async_copy(dcyc.at[other], dcyc.at[other], grecv.at[other]).wait()

    def row_step(step, carry):
        slot = lax.rem(step, 2)

        @pl.when(step + 1 < n_row)
        def _():
            row_load(step + 1, 1 - slot).start()

        row_load(step, slot).wait()
        dhid_ref[:, pl.ds(pl.multiple_of(step * th, th), th)] = lax.dot_general(
            dcyc[...].reshape(n_sp * slot_rows, width), wrow[slot], (((1,), (1,)), ((), ())),
            preferred_element_type=jnp.float32,
        )
        return carry

    lax.fori_loop(0, n_row, row_step, 0)

    for step in range(2, chips):
        relay(step)

    for index in range(chips):
        h_wait(index * 2 + 1 - core)
    for off in range(1, n_sp):
        other = lax.rem(sp + off, n_sp)
        pltpu.make_async_copy(dall_ref.at[:, other], dall_ref.at[:, other], brecv.at[other]).wait()

    def drain(step, carry):
        cols = pl.ds(pl.multiple_of(step * tn, tn), tn)
        for off in range(1, n_sp):
            other = lax.rem(sp + off, n_sp)
            r_send(step, off).wait_send()
            pltpu.make_async_copy(rs_ref.at[other, :, cols], rs_ref.at[other, :, cols], rrecv.at[step, other]).wait()
        return carry

    lax.fori_loop(0, n_col, drain, 0)
    own_part.wait()
    for off in range(1, n_sp):
        g_send(off).wait_send()
        b_send(off).wait_send()
    for off in range(1, n_dp):
        a_send(off).wait_send()
    for step in range(chips):
        src = hid_ref if step == 0 else None

        @pl.when((chip - step >= 0) & (chip + 1 < chips))
        def _():
            index = (chip - step) * 2 + core
            h_send(index, hid_ref if step == 0 else h_block(index), chip + 1, right_send.at[step]).wait_send()

        @pl.when((chip + step < chips) & (chip >= 1))
        def _():
            index = (chip + step) * 2 + core
            h_send(index, hid_ref if step == 0 else h_block(index), chip - 1, left_send.at[step]).wait_send()

        h_pair(dp, hid_ref, pair_send.at[step]).wait_send()


def exchange(n_dp, n_sp, hidden, d_slot, w_down):
    slots, hid_width = hidden.shape
    slot_rows, width = d_slot.shape
    block = width // n_dp
    tn, th = width // 8, min(256, hid_width)
    n_col = width // tn
    chips = n_dp // 2
    bf = jnp.bfloat16
    dma = pltpu.SemaphoreType.DMA
    hbm = pl.BlockSpec(memory_space=pl.ANY)
    vmem = pl.BlockSpec(memory_space=pltpu.VMEM)
    return pl.pallas_call(
        functools.partial(exchange_kernel, n_dp, n_sp),
        out_shape=(
            jax.ShapeDtypeStruct((n_sp, slot_rows, width), bf),
            jax.ShapeDtypeStruct((slots, hid_width), jnp.float32),
            jax.ShapeDtypeStruct((n_dp, slots, hid_width), bf),
            jax.ShapeDtypeStruct((n_dp, n_sp, slot_rows, block), bf),
        ),
        in_specs=[vmem, vmem, hbm],
        out_specs=(hbm, vmem, hbm, hbm),
        scratch_shapes=[
            pltpu.VMEM((n_sp, slot_rows, width), bf),
            pltpu.VMEM((n_sp, slot_rows, width), bf),
            pltpu.VMEM((2, hid_width, tn), bf),
            pltpu.VMEM((2, th, width), bf),
            dma((4,)),
            dma((4,)),
            dma((chips,)),
            dma((chips,)),
            dma((chips,)),
            dma((n_dp,)),
            dma((n_dp,)),
            dma((n_dp,)),
            dma((n_sp,)),
            dma((n_sp,)),
            dma((n_sp,)),
            dma((n_sp,)),
            dma((n_col, n_sp)),
            dma((n_col, n_sp)),
        ],
        compiler_params=pltpu.CompilerParams(
            collective_id=0, has_side_effects=True, vmem_limit_bytes=60 * 1024 * 1024
        ),
    )(hidden, d_slot, w_down)


def contract_rows(left, right):
    return lax.dot_general(
        left, right, (((0,), (0,)), ((), ())), preferred_element_type=jnp.float32
    )


def local(n_dp, n_sp, gate_pre, up_pre, w_down, route_logits, expert_ids, d_out):
    tok_rows = expert_ids.shape[0]
    slot_rows = tok_rows // 2
    routed = jnp.any(expert_ids == 0, axis=1)
    routed_int = routed.astype(jnp.int32)
    routed_float = routed.astype(jnp.float32)
    slot_rank = jnp.cumsum(routed_int) - 1
    gate_wide = gate_pre.astype(jnp.float32)
    up_wide = up_pre.astype(jnp.float32)
    sigma_gate = jax.nn.sigmoid(gate_wide)
    silu_gate = gate_wide * sigma_gate
    hidden = (silu_gate * up_wide).astype(jnp.bfloat16)
    first_zero = expert_ids[:, 0] == 0
    own_logit = jnp.where(first_zero, route_logits[:, 0], route_logits[:, 1])
    other_logit = jnp.where(first_zero, route_logits[:, 1], route_logits[:, 0])
    weight_zero = routed_float * jax.nn.sigmoid(own_logit - other_logit)
    chooser = (slot_rank[:, None] == jnp.arange(slot_rows, dtype=jnp.int32)[None, :]) & routed[
        :, None
    ]
    picked = contract_rows(chooser.astype(jnp.bfloat16), d_out)
    slot_weight = jnp.sum(jnp.where(chooser, weight_zero[:, None], 0.0), axis=0)
    d_slot = (slot_weight[:, None] * picked).astype(jnp.bfloat16)
    pieces, d_hidden, hidden_all, d_all = exchange(n_dp, n_sp, hidden, d_slot, w_down)
    expert_out = jnp.sum(pieces.astype(jnp.float32), axis=0)
    safe_rank = jnp.clip(slot_rank, 0, slot_rows - 1)
    token_out = expert_out[safe_rank] * routed_float[:, None]
    mixed = (weight_zero[:, None] * token_out).astype(jnp.bfloat16)
    weight_grad = jnp.sum(d_out.astype(jnp.float32) * token_out, axis=1)
    logit_grad = weight_grad * weight_zero * (1.0 - weight_zero)
    first_col = jnp.where(first_zero, logit_grad, -logit_grad)
    logit_grads = jnp.stack([first_col, -first_col], axis=1)
    down_grads = contract_rows(
        hidden_all.reshape(-1, hidden_all.shape[-1]), d_all.reshape(-1, d_all.shape[-1])
    )
    gate_grads = (d_hidden * up_wide * sigma_gate * (1.0 + gate_wide * (1.0 - sigma_gate))).astype(
        jnp.bfloat16
    )
    up_grads = (d_hidden * silu_gate).astype(jnp.bfloat16)
    return (mixed, logit_grads, gate_grads, up_grads, down_grads)


def solution(mesh):
    both = P(("dp", "sp"), None)
    return jax.shard_map(
        functools.partial(local, mesh.shape["dp"], mesh.shape["sp"]),
        mesh=mesh,
        in_specs=(P("dp", "sp"), P("dp", "sp"), P("sp", None), both, both, both),
        out_specs=(both, both, P("dp", "sp"), P("dp", "sp"), P("sp", "dp")),
        check_vma=False,
    )
```

time: 290 us -> 144 us (0.50)
  waiting for transfers between devices: 213 us -> 0 us
  Pallas kernels: 0 us -> 113 us
  matrix products: 41.3 us -> 13.5 us
  between operations: 13.8 us -> 0.72 us
  starting transfers between devices: 5.04 us -> 0 us
  other arithmetic: 8.3 us -> 12.9 us
  local copies, waits for them, and re-layouts: 7.69 us -> 3.39 us
    all_gather x2 -> x0, waiting for transfers between devices: 167 us -> none  [the longest x1 124 us: local(): lax.all_gather(hidden, 'dp', axis=0, tiled=True)]
    pallas_call x0 -> x1, Pallas kernels: none -> 113 us  [exchange(): pl.pallas_call(functools.partial(exchange_kernel, n_dp, n_sp), out_shape=...]
    reduce_scatter x1 -> x0, waiting for transfers between devices: 45.7 us -> none  [local(): lax.psum_scatter(plain_product(hidden, w_down).astype(jnp.bfloat16), 'sp'...]
    dot_general x3 -> x0, matrix products: 28 us -> none  [the longest x1 14.7 us: contract_cols(): lax.dot_general(left, right, (((1,), (1,)), ((), ())), preferred_element_...]
    all_to_all x1 -> x0, starting transfers between devices: 4.92 us -> none  [local(): lax.all_to_all(extra_part, 'dp', split_axis=1, concat_axis=0, tiled=True)]
    all_to_all x1 -> x0, local copies, waits for them, and re-layouts: 3.72 us -> none  [local(): lax.all_to_all(extra_part, 'dp', split_axis=1, concat_axis=0, tiled=True)]
  transfers between devices with their start and end apart: 4 -> 0, of which waited for: 3 -> 0; matrix products, arithmetic and copies ran while one was open for 7% -> 0% of each run, Pallas kernels for 0% -> 0%
where the time goes in v1:
time: 144 us
  Pallas kernels  113 us (78%)
  matrix products  13.5 us (9%)
  other arithmetic  12.9 us (9%)
  local copies, waits for them, and re-layouts  3.39 us (2%)
    pallas_call x1, Pallas kernels, exchange(): pl.pallas_call(functools.partial(exchange_kernel, n_dp, n_sp), out_shape=...  113 us
    dot_general x2, matrix products, contract_rows(): lax.dot_general(left, right, (((0,), (0,)), ((), ())), preferred_element_...  13.5 us
    reduce_sum x1, other arithmetic, local(): weight_grad = jnp.sum(d_out.astype(jnp.float32) * token_out, axis=1)  3.89 us
    gather x1, local copies, waits for them, and re-layouts, local(): token_out = expert_out[safe_rank] * routed_float[:, None]  3.17 us

profile of v1, /device:TPU:0, one launch (start us, length us, event | category | flops | bytes accessed | tf_op | source)
XLA Modules:
  0.0 143.8 jit_solution(13732313904024560968)
XLA Ops:
  0.6 0.0 copy-start.1
  0.6 0.0 copy-start.3
  0.7 0.8 compare_reduce_fusion
  1.5 0.8 bitcast_select_fusion
  2.3 0.1 copy.61
  2.4 0.2 reduce-window.4
  2.6 0.1 copy.62
  2.6 0.1 select_reduce_fusion
  2.8 2.6 %fusion.dslot_ref = bf16[64,6144]{1,0:T(8,128)(2,1)} fusion(bf16[128,6144]{1,0:T(8,128)(2,1)} %param.11, f32[64]{0:T(128)S(1)} %select_reduce_fusion, s32[128]{0:T(128)S(1)} %get-tuple-element.32, pred[128]{0:T(512)(128)(4,1)S(1)} %compare_reduce_fusion), kind=kOutput, calls=%fused_computation.2 | convolution fusion | flops 101466112 | bytes 2360192 | tf_op jit(solution)/shard_map/dot_general | solution.py:276
  5.4 0.0 copy-done.1
  5.4 0.0 copy-done.3
  5.4 1.7 %fusion.1.hid_ref = bf16[256,2048]{1,0:T(8,128)(2,1)} fusion(bf16[256,2048]{1,0:T(8,128)(2,1)S(1)} %copy-done.1, bf16[256,2048]{1,0:T(8,128)(2,1)S(1)} %copy-done.3), kind=kLoop, calls=%fused_computation.11 | loop fusion | flops 4194304 | bytes 3145728 | tf_op jit(solution)/shard_map/convert_element_type | solution.py:292
  7.1 113.2 %shard_map.101 = (bf16[4,64,6144]{2,1,0:T(8,128)(2,1)}, f32[256,2048]{1,0:T(8,128)}, bf16[8,256,2048]{2,1,0:T(8,128)(2,1)}, bf16[8,4,64,768]{3,2,1,0:T(8,128)(2,1)}) custom-call(bf16[256,2048]{1,0:T(8,128)(2,1)} %fusion.1.hid_ref, bf16[64,6144]{1,0:T(8,128)(2,1)} %fusion.dslot_ref, bf16[2048,6144]{1,0:T(8,128)(2,1)} %w_ref.1), custom_call_target="tpu_custom_call" | custom-call | tf_op jit(solution)/shard_map/pallas_call | solution.py:239
  120.3 2.5 %convert_reduce_fusion = f32[64,6144]{1,0:T(8,128)S(1)} fusion(bf16[4,64,6144]{2,1,0:T(8,128)(2,1)} %get-tuple-element.9), kind=kLoop, calls=%fused_computation.3 | loop fusion | flops 2752512 | bytes 4718592 | tf_op jit(solution)/shard_map/reduce_sum | solution.py:304
  122.9 0.0 copy-start
  122.9 3.2 %gather_fusion = f32[128,6144]{1,0:T(8,128)} fusion(f32[64,6144]{1,0:T(8,128)S(1)} %convert_reduce_fusion, s32[1024]{0:T(1024)S(1)} %pad_clamp_fusion), kind=kCustom, calls=%fused_computation | custom fusion | bytes 6291968 | tf_op jit(solution)/shard_map/gather | solution.py:306
  126.1 0.0 copy-done
  126.1 0.0 copy-start.5
  126.1 0.0 copy-start.7
  126.1 3.9 %multiply_reduce_fusion = (f32[128]{0:T(128)S(1)}, bf16[128,6144]{1,0:T(8,128)(2,1)}) fusion(bf16[128,6144]{1,0:T(8,128)(2,1)S(1)} %copy-done, f32[128,6144]{1,0:T(8,128)} %gather_fusion, f32[128]{0:T(128)S(1)} %get-tuple-element.29, f32[128]{0:T(128)S(1)} %bitcast.21), kind=kLoop, calls=%fused_computation.4 | loop fusion | flops 4718464 | bytes 6292992 | tf_op jit(solution)/shard_map/reduce_sum | solution.py:308
  130.0 0.6 pad_maximum_fusion
  130.6 0.0 copy-done.4
  130.6 2.3 %multiply_convert_fusion.1 = (bf16[256,2048]{1,0:T(8,128)(2,1)}, bf16[256,2048]{1,0:T(8,128)(2,1)}) fusion(f32[256,2048]{1,0:T(8,128)S(1)} %copy-done.5, bf16[256,2048]{1,0:T(8,128)(2,1)S(1)} %copy-done.4, bf16[256,2048]{1,0:T(8,128)(2,1)S(1)} %copy-done.2), kind=kLoop, calls=%fused_computation.19 | loop fusion | flops 7864320 | bytes 6291456 | tf_op jit(solution)/shard_map/convert_element_type | solution.py:318
  132.9 10.8 %fusion.17 = f32[2048,768]{1,0:T(8,128)} fusion(bf16[2048,2048]{1,0:T(8,128)(2,1)S(1)} %bitcast.22, bf16[2048,768]{1,0:T(8,128)(2,1)} %bitcast.23), kind=kOutput, calls=%fused_computation.38 | convolution fusion | flops 6442450944 | bytes 17825792 | tf_op jit(solution)/shard_map/dot_general | solution.py:276
  (11 shorter events, 0.0 us)
Async XLA Ops:
  0.6 4.8 %copy-start.1 = (bf16[256,2048]{1,0:T(8,128)(2,1)S(1)}, bf16[256,2048]{1,0:T(8,128)(2,1)}, u32[]{:S(2)}) copy-start(bf16[256,2048]{1,0:T(8,128)(2,1)} %param.7) | copy-start | bytes 3145732
  0.6 4.8 %copy-start.3 = (bf16[256,2048]{1,0:T(8,128)(2,1)S(1)}, bf16[256,2048]{1,0:T(8,128)(2,1)}, u32[]{:S(2)}) copy-start(bf16[256,2048]{1,0:T(8,128)(2,1)} %param.6) | copy-start | bytes 3145732
  122.9 3.2 %copy-start = (bf16[128,6144]{1,0:T(8,128)(2,1)S(1)}, bf16[128,6144]{1,0:T(8,128)(2,1)}, u32[]{:S(2)}) copy-start(bf16[128,6144]{1,0:T(8,128)(2,1)} %param.11) | copy-start | bytes 4718596
  126.1 3.9 %copy-start.6 = (s32[128,2]{0,1:T(2,128)S(1)}, s32[128,2]{0,1:T(2,128)}, u32[]{:S(2)}) copy-start(s32[128,2]{0,1:T(2,128)} %param.10) | copy-start | bytes 3076
  126.1 4.5 %copy-start.2 = (bf16[256,2048]{1,0:T(8,128)(2,1)S(1)}, bf16[256,2048]{1,0:T(8,128)(2,1)}, u32[]{:S(2)}) copy-start(bf16[256,2048]{1,0:T(8,128)(2,1)} %param.7) | copy-start | bytes 3145732
  126.1 4.5 %copy-start.4 = (bf16[256,2048]{1,0:T(8,128)(2,1)S(1)}, bf16[256,2048]{1,0:T(8,128)(2,1)}, u32[]{:S(2)}) copy-start(bf16[256,2048]{1,0:T(8,128)(2,1)} %param.6) | copy-start | bytes 3145732
  126.1 4.5 %copy-start.5 = (f32[256,2048]{1,0:T(8,128)S(1)}, f32[256,2048]{1,0:T(8,128)}, u32[]{:S(2)}) copy-start(f32[256,2048]{1,0:T(8,128)} %get-tuple-element.10) | copy-start | bytes 6291460
  126.1 6.8 %copy-start.7 = (bf16[8,256,2048]{2,1,0:T(8,128)(2,1)S(1)}, bf16[8,256,2048]{2,1,0:T(8,128)(2,1)}, u32[]{:S(2)}) copy-start(bf16[8,256,2048]{2,1,0:T(8,128)(2,1)} %get-tuple-element.11) | copy-start | bytes 25165828

commit v2 on v1

--- a/solution.py
+++ b/solution.py
@@ -11,9 +11,10 @@
 
 
 def exchange_kernel(
-    n_dp, n_sp, hid_ref, dslot_ref, w_ref, rs_ref, dhid_ref, hall_ref, dall_ref,
-    part, dcyc, wcol, wrow, wsem, local_sem,
-    right_send, left_send, pair_send, hrecv, asend, arecv, gsend, grecv, bsend, brecv, rsend, rrecv,
+    n_dp, n_sp, hid_ref, dslot_ref, w_ref, choose_ref, weight_ref, dout_ref,
+    dhid_ref, hall_ref, dall_ref, mixed_ref, wgrad_ref,
+    part, rs_ref, dcyc, wcol, wrow, wsem, local_sem,
+    right_send, left_send, pair_send, hrecv, asend, arecv, gsend, grecv, bsend, brecv, rsend, rrecv, fsend, frecv,
 ):
     dp, sp = lax.axis_index("dp"), lax.axis_index("sp")
     chips = n_dp // 2
@@ -86,11 +87,39 @@
 
     h_pair(dp, hid_ref, pair_send.at[chip]).start()
 
-    def g_send(off):
-        return remote(dslot_ref, dcyc.at[sp], gsend.at[off], grecv.at[sp], sp=lax.rem(sp + off, n_sp))
-
-    for off in range(1, n_sp):
-        g_send(off).start()
+    relayed = n_sp == 4
+    if relayed:
+        near = [sp + 1 - 2 * lax.rem(sp, 2), lax.rem(sp + 2, 4)]
+    else:
+        near = [lax.rem(sp + off, n_sp) for off in range(1, n_sp)]
+    half_rows, half_dp = slot_rows // 2, n_dp // 2
+
+    def g_send(way):
+        return remote(dslot_ref, dcyc.at[sp], gsend.at[way], grecv.at[sp], sp=near[way])
+
+    def b_send(way):
+        return remote(dall_ref.at[:, sp], dall_ref.at[:, sp], bsend.at[way], brecv.at[sp], sp=near[way])
+
+    def g_half(source, way):
+        return dcyc.at[source, way * half_rows:(way + 1) * half_rows]
+
+    def b_half(source, way):
+        return dall_ref.at[way * half_dp:(way + 1) * half_dp, source]
+
+    def g_pass(way):
+        held = g_half(near[way], way)
+        return remote(held, held, fsend.at[way], frecv.at[way], sp=near[1 - way])
+
+    def b_pass(way):
+        held = b_half(near[way], way)
+        return remote(held, held, fsend.at[2 + way], frecv.at[2 + way], sp=near[1 - way])
+
+    def arrived(ref, sem):
+        pltpu.make_async_copy(ref, ref, sem).wait()
+
+    ways = range(len(near))
+    for way in ways:
+        g_send(way).start()
 
     own = [
         pltpu.make_async_copy(dslot_ref, dcyc.at[sp], local_sem.at[0]),
@@ -126,19 +155,18 @@
         return carry
 
     lax.fori_loop(0, n_col, col_step, 0)
-    own_part = pltpu.make_async_copy(part.at[sp], rs_ref.at[sp], local_sem.at[3])
-    own_part.start()
+    for way in ways:
+        arrived(dcyc.at[near[way]], grecv.at[near[way]])
+        if relayed:
+            g_pass(way).start()
 
     for copy in own:
         copy.wait()
     for off in range(1, n_dp):
         a_wait(off)
 
-    def b_send(off):
-        return remote(dall_ref.at[:, sp], dall_ref.at[:, sp], bsend.at[off], brecv.at[sp], sp=lax.rem(sp + off, n_sp))
-
-    for off in range(1, n_sp):
-        b_send(off).start()
+    for way in ways:
+        b_send(way).start()
 
     def relay(step):
         @pl.when(chip - step >= 0)
@@ -163,11 +191,12 @@
 
             h_pair(index, h_block(index), pair_send.at[chip + step]).start()
 
-    relay(1)
-
-    for off in range(1, n_sp):
-        other = lax.rem(sp + off, n_sp)
-        pltpu.make_async_copy(dcyc.at[other], dcyc.at[other], grecv.at[other]).wait()
+    for step in range(1, min(3, chips)):
+        relay(step)
+
+    if relayed:
+        for way in ways:
+            arrived(g_half(3 - sp, way), frecv.at[way])
 
     def row_step(step, carry):
         slot = lax.rem(step, 2)
@@ -185,32 +214,48 @@
 
     lax.fori_loop(0, n_row, row_step, 0)
 
-    for step in range(2, chips):
+    wgrad_ref[...] = jnp.zeros_like(wgrad_ref)
+
+    def mix_step(step, carry):
+        cols = pl.ds(pl.multiple_of(step * tn, tn), tn)
+        total = part[sp, :, cols].astype(jnp.float32)
+        for off in range(1, n_sp):
+            other = lax.rem(sp + off, n_sp)
+            arrived(rs_ref.at[other, :, cols], rrecv.at[step, other])
+            total = total + rs_ref[other, :, cols].astype(jnp.float32)
+        high = total.astype(jnp.bfloat16)
+        low = (total - high.astype(jnp.float32)).astype(jnp.bfloat16)
+        token_out = jnp.dot(choose_ref[...], high, preferred_element_type=jnp.float32) + jnp.dot(
+            choose_ref[...], low, preferred_element_type=jnp.float32
+        )
+        mixed_ref[:, cols] = (weight_ref[...] * token_out).astype(jnp.bfloat16)
+        wgrad_ref[...] += jnp.sum(dout_ref[:, cols].astype(jnp.float32) * token_out, axis=1, keepdims=True)
+        for off in range(1, n_sp):
+            r_send(step, off).wait_send()
+        return carry
+
+    lax.fori_loop(0, n_col, mix_step, 0)
+
+    for way in ways:
+        arrived(dall_ref.at[:, near[way]], brecv.at[near[way]])
+        if relayed:
+            b_pass(way).start()
+
+    for step in range(3, chips):
         relay(step)
 
     for index in range(chips):
         h_wait(index * 2 + 1 - core)
-    for off in range(1, n_sp):
-        other = lax.rem(sp + off, n_sp)
-        pltpu.make_async_copy(dall_ref.at[:, other], dall_ref.at[:, other], brecv.at[other]).wait()
-
-    def drain(step, carry):
-        cols = pl.ds(pl.multiple_of(step * tn, tn), tn)
-        for off in range(1, n_sp):
-            other = lax.rem(sp + off, n_sp)
-            r_send(step, off).wait_send()
-            pltpu.make_async_copy(rs_ref.at[other, :, cols], rs_ref.at[other, :, cols], rrecv.at[step, other]).wait()
-        return carry
-
-    lax.fori_loop(0, n_col, drain, 0)
-    own_part.wait()
-    for off in range(1, n_sp):
-        g_send(off).wait_send()
-        b_send(off).wait_send()
+    for way in ways:
+        g_send(way).wait_send()
+        b_send(way).wait_send()
+        if relayed:
+            arrived(b_half(3 - sp, way), frecv.at[2 + way])
+            g_pass(way).wait_send()
+            b_pass(way).wait_send()
     for off in range(1, n_dp):
         a_send(off).wait_send()
     for step in range(chips):
-        src = hid_ref if step == 0 else None
 
         @pl.when((chip - step >= 0) & (chip + 1 < chips))
         def _():
@@ -225,7 +270,7 @@
         h_pair(dp, hid_ref, pair_send.at[step]).wait_send()
 
 
-def exchange(n_dp, n_sp, hidden, d_slot, w_down):
+def exchange(n_dp, n_sp, hidden, d_slot, w_down, choose, weight, d_out):
     slots, hid_width = hidden.shape
     slot_rows, width = d_slot.shape
     block = width // n_dp
@@ -239,14 +284,16 @@
     return pl.pallas_call(
         functools.partial(exchange_kernel, n_dp, n_sp),
         out_shape=(
-            jax.ShapeDtypeStruct((n_sp, slot_rows, width), bf),
             jax.ShapeDtypeStruct((slots, hid_width), jnp.float32),
             jax.ShapeDtypeStruct((n_dp, slots, hid_width), bf),
             jax.ShapeDtypeStruct((n_dp, n_sp, slot_rows, block), bf),
+            jax.ShapeDtypeStruct(d_out.shape, bf),
+            jax.ShapeDtypeStruct((d_out.shape[0], 1), jnp.float32),
         ),
-        in_specs=[vmem, vmem, hbm],
-        out_specs=(hbm, vmem, hbm, hbm),
+        in_specs=[vmem, vmem, hbm, vmem, vmem, vmem],
+        out_specs=(vmem, hbm, hbm, vmem, vmem),
         scratch_shapes=[
+            pltpu.VMEM((n_sp, slot_rows, width), bf),
             pltpu.VMEM((n_sp, slot_rows, width), bf),
             pltpu.VMEM((n_sp, slot_rows, width), bf),
             pltpu.VMEM((2, hid_width, tn), bf),
@@ -265,11 +312,13 @@
             dma((n_sp,)),
             dma((n_col, n_sp)),
             dma((n_col, n_sp)),
+            dma((4,)),
+            dma((4,)),
         ],
         compiler_params=pltpu.CompilerParams(
             collective_id=0, has_side_effects=True, vmem_limit_bytes=60 * 1024 * 1024
         ),
-    )(hidden, d_slot, w_down)
+    )(hidden, d_slot, w_down, choose, weight, d_out)
 
 
 def contract_rows(left, right):
@@ -300,13 +349,10 @@
     picked = contract_rows(chooser.astype(jnp.bfloat16), d_out)
     slot_weight = jnp.sum(jnp.where(chooser, weight_zero[:, None], 0.0), axis=0)
     d_slot = (slot_weight[:, None] * picked).astype(jnp.bfloat16)
-    pieces, d_hidden, hidden_all, d_all = exchange(n_dp, n_sp, hidden, d_slot, w_down)
-    expert_out = jnp.sum(pieces.astype(jnp.float32), axis=0)
-    safe_rank = jnp.clip(slot_rank, 0, slot_rows - 1)
-    token_out = expert_out[safe_rank] * routed_float[:, None]
-    mixed = (weight_zero[:, None] * token_out).astype(jnp.bfloat16)
-    weight_grad = jnp.sum(d_out.astype(jnp.float32) * token_out, axis=1)
-    logit_grad = weight_grad * weight_zero * (1.0 - weight_zero)
+    d_hidden, hidden_all, d_all, mixed, weight_grad = exchange(
+        n_dp, n_sp, hidden, d_slot, w_down, chooser.astype(jnp.bfloat16), weight_zero[:, None], d_out
+    )
+    logit_grad = weight_grad[:, 0] * weight_zero * (1.0 - weight_zero)
     first_col = jnp.where(first_zero, logit_grad, -logit_grad)
     logit_grads = jnp.stack([first_col, -first_col], axis=1)
     down_grads = contract_rows(

time: 144 us -> 129 us (0.90)
  Pallas kernels: 113 us -> 101 us
  other arithmetic: 12.9 us -> 10.6 us
    pallas_call x1, Pallas kernels: 113 us -> 101 us  [exchange(): pl.pallas_call(functools.partial(exchange_kernel, n_dp, n_sp), out_shape=...]
    reduce_sum x2 -> x0, other arithmetic: 6.43 us -> none  [the longest x1 3.89 us: local(): weight_grad = jnp.sum(d_out.astype(jnp.float32) * token_out, axis=1)]
    gather x1 -> x0, local copies, waits for them, and re-layouts: 3.17 us -> none  [local(): token_out = expert_out[safe_rank] * routed_float[:, None]]
    convert_element_type x1, other arithmetic: 2.35 us -> 4.12 us  [local(): up_grads = (d_hidden * silu_gate).astype(jnp.bfloat16)]
where the time goes in v2:
time: 129 us
  Pallas kernels  101 us (78%)
  matrix products  13.9 us (11%)
  other arithmetic  10.6 us (8%)
  local copies, waits for them, and re-layouts  2.67 us (2%)
    pallas_call x1, Pallas kernels, exchange(): pl.pallas_call(functools.partial(exchange_kernel, n_dp, n_sp), out_shape=...  101 us
    dot_general x2, matrix products, contract_rows(): lax.dot_general(left, right, (((0,), (0,)), ((), ())), preferred_element_...  13.9 us
    convert_element_type x1, other arithmetic, local(): up_grads = (d_hidden * silu_gate).astype(jnp.bfloat16)  4.12 us

profile of v2, /device:TPU:0, one launch (start us, length us, event | category | flops | bytes accessed | tf_op | source)
XLA Modules:
  0.0 128.9 jit_solution(9750002198807132504)
XLA Ops:
  0.6 0.0 copy-start
  0.7 0.8 compare_reduce_fusion
  1.5 0.7 slice_compare_fusion
  2.2 0.8 fusion.16
  2.9 0.1 copy.46
  3.1 0.1 copy.52
  3.2 0.1 copy.47
  3.3 0.1 copy.45
  3.4 0.2 reduce-window.8
  3.6 0.1 add_reduce_fusion
  3.7 0.7 fusion.10.choose_ref
  4.5 0.1 copy.48
  4.6 0.7 fusion.15
  5.2 0.1 select_reduce_fusion
  5.4 2.8 %fusion.dslot_ref = bf16[64,6144]{1,0:T(8,128)(2,1)} fusion(bf16[128,6144]{1,0:T(8,128)(2,1)} %dout_ref.1, f32[64]{0:T(128)S(1)} %select_reduce_fusion, s32[128]{0:T(128)S(1)} %add_reduce_fusion, pred[128]{0:T(512)(128)(4,1)S(1)} %compare_reduce_fusion), kind=kOutput, calls=%fused_computation.1 | convolution fusion | flops 101466112 | bytes 2360192 | tf_op jit(solution)/shard_map/dot_general | solution.py:325
  8.2 1.7 %fusion.1.hid_ref = bf16[256,2048]{1,0:T(8,128)(2,1)} fusion(bf16[256,2048]{1,0:T(8,128)(2,1)S(1)} %copy-done, bf16[256,2048]{1,0:T(8,128)(2,1)S(1)} %copy-done.1), kind=kLoop, calls=%fused_computation.7 | loop fusion | flops 4194304 | bytes 3145728 | tf_op jit(solution)/shard_map/convert_element_type | solution.py:341
  9.8 101.1 %shard_map.101 = (f32[256,2048]{1,0:T(8,128)}, bf16[8,256,2048]{2,1,0:T(8,128)(2,1)}, bf16[8,4,64,768]{3,2,1,0:T(8,128)(2,1)}, bf16[128,6144]{1,0:T(8,128)(2,1)}, f32[128,1]{1,0:T(8,128)}) custom-call(bf16[256,2048]{1,0:T(8,128)(2,1)} %fusion.1.hid_ref, bf16[64,6144]{1,0:T(8,128)(2,1)} %fusion.dslot_ref, bf16[2048,6144]{1,0:T(8,128)(2,1)} %w_ref.1, ...), custom_call_target="tpu_custom_call" | custom-call | tf_op jit(solution)/shard_map/pallas_call | solution.py:284
  110.9 0.9 fusion.14
  111.8 0.1 copy.55
  111.8 0.1 copy.54
  111.9 0.6 pad_maximum_fusion
  112.5 4.1 %multiply_convert_fusion = (bf16[256,2048]{1,0:T(8,128)(2,1)}, bf16[256,2048]{1,0:T(8,128)(2,1)}) fusion(f32[256,2048]{1,0:T(8,128)} %get-tuple-element.12, bf16[256,2048]{1,0:T(8,128)(2,1)S(1)} %copy-done.1, bf16[256,2048]{1,0:T(8,128)(2,1)S(1)} %copy-done), kind=kLoop, calls=%fused_computation.15 | loop fusion | flops 7864320 | bytes 6291456 | tf_op jit(solution)/shard_map/convert_element_type | solution.py:364
  116.6 11.1 %fusion.17 = f32[2048,768]{1,0:T(8,128)} fusion(bf16[2048,2048]{1,0:T(8,128)(2,1)} %bitcast.8, bf16[2048,768]{1,0:T(8,128)(2,1)S(1)} %bitcast.9), kind=kOutput, calls=%fused_computation.32 | convolution fusion | flops 6442450944 | bytes 17825792 | tf_op jit(solution)/shard_map/dot_general | solution.py:325
  127.7 1.1 copy.57
  (10 shorter events, 0.0 us)
Async XLA Ops:
  0.6 7.5 %copy-start = (bf16[256,2048]{1,0:T(8,128)(2,1)S(1)}, bf16[256,2048]{1,0:T(8,128)(2,1)}, u32[]{:S(2)}) copy-start(bf16[256,2048]{1,0:T(8,128)(2,1)} %param.7) | copy-start | bytes 3145732
  0.6 7.5 %copy-start.1 = (bf16[256,2048]{1,0:T(8,128)(2,1)S(1)}, bf16[256,2048]{1,0:T(8,128)(2,1)}, u32[]{:S(2)}) copy-start(bf16[256,2048]{1,0:T(8,128)(2,1)} %param.6) | copy-start | bytes 3145732
  9.8 101.1 %copy-start.3 = (f32[128,1]{1,0:T(8,128)S(1)}, f32[128,1]{1,0:T(8,128)}, u32[]{:S(2)}) copy-start(f32[128,1]{1,0:T(8,128)} %get-tuple-element.28.weight_ref) | copy-start | bytes 1540
  112.5 4.1 %copy-start.4 = (bf16[8,4,64,768]{3,2,1,0:T(8,128)(2,1)S(1)}, bf16[8,4,64,768]{3,2,1,0:T(8,128)(2,1)}, u32[]{:S(2)}) copy-start(bf16[8,4,64,768]{3,2,1,0:T(8,128)(2,1)} %get-tuple-element.14) | copy-start | bytes 9437188
  116.6 11.1 %copy-start.2 = (bf16[128,6144]{1,0:T(8,128)(2,1)S(1)}, bf16[128,6144]{1,0:T(8,128)(2,1)}, u32[]{:S(2)}) copy-start(bf16[128,6144]{1,0:T(8,128)(2,1)} %get-tuple-element.38) | copy-start | bytes 4718596

commit v3 on v2

--- a/solution.py
+++ b/solution.py
@@ -139,6 +139,31 @@
             rsend.at[step, off], rrecv.at[step, sp], sp=other,
         )
 
+    def half_cols(step, way):
+        half = tn // 2
+        return pl.ds(pl.multiple_of(step * tn + way * half, half), half)
+
+    def r_hop(step, way, kind):
+        cols = half_cols(step, way)
+        src = [part.at[near[way], :, cols], part.at[3 - sp, :, cols], rs_ref.at[3, :, cols]][kind]
+        return remote(
+            src, rs_ref.at[kind, :, cols], rsend.at[step, 2 * kind + way], rrecv.at[step, 2 * kind + way],
+            sp=near[1 - way if kind == 2 else way],
+        )
+
+    def r_arrived(step, way, kind):
+        arrived(rs_ref.at[kind, :, half_cols(step, way)], rrecv.at[step, 2 * kind + way])
+
+    def fold_step(step, carry):
+        for way in range(2):
+            cols = half_cols(step, way)
+            r_arrived(step, way, 1)
+            rs_ref[3, :, cols] = (
+                part[near[1 - way], :, cols].astype(jnp.float32) + rs_ref[1, :, cols].astype(jnp.float32)
+            ).astype(jnp.bfloat16)
+            r_hop(step, way, 2).start()
+        return carry
+
     def col_step(step, carry):
         slot = lax.rem(step, 2)
 
@@ -150,8 +175,13 @@
         cols = pl.ds(pl.multiple_of(step * tn, tn), tn)
         product = jnp.dot(hid_ref[...], wcol[slot], preferred_element_type=jnp.float32)
         part[:, :, cols] = product.astype(jnp.bfloat16).reshape(n_sp, slot_rows, tn)
-        for off in range(1, n_sp):
-            r_send(step, off).start()
+        if relayed:
+            for kind in (1, 0):
+                for way in range(2):
+                    r_hop(step, way, kind).start()
+        else:
+            for off in range(1, n_sp):
+                r_send(step, off).start()
         return carry
 
     lax.fori_loop(0, n_col, col_step, 0)
@@ -191,10 +221,11 @@
 
             h_pair(index, h_block(index), pair_send.at[chip + step]).start()
 
-    for step in range(1, min(3, chips)):
+    for step in range(1, min(2, chips)):
         relay(step)
 
     if relayed:
+        lax.fori_loop(0, n_col, fold_step, 0)
         for way in ways:
             arrived(g_half(3 - sp, way), frecv.at[way])
 
@@ -214,15 +245,24 @@
 
     lax.fori_loop(0, n_row, row_step, 0)
 
+    for step in range(2, min(3, chips)):
+        relay(step)
+
     wgrad_ref[...] = jnp.zeros_like(wgrad_ref)
 
     def mix_step(step, carry):
         cols = pl.ds(pl.multiple_of(step * tn, tn), tn)
         total = part[sp, :, cols].astype(jnp.float32)
-        for off in range(1, n_sp):
-            other = lax.rem(sp + off, n_sp)
-            arrived(rs_ref.at[other, :, cols], rrecv.at[step, other])
-            total = total + rs_ref[other, :, cols].astype(jnp.float32)
+        if relayed:
+            for kind in (0, 2):
+                for way in range(2):
+                    r_arrived(step, way, kind)
+                total = total + rs_ref[kind, :, cols].astype(jnp.float32)
+        else:
+            for off in range(1, n_sp):
+                other = lax.rem(sp + off, n_sp)
+                arrived(rs_ref.at[other, :, cols], rrecv.at[step, other])
+                total = total + rs_ref[other, :, cols].astype(jnp.float32)
         high = total.astype(jnp.bfloat16)
         low = (total - high.astype(jnp.float32)).astype(jnp.bfloat16)
         token_out = jnp.dot(choose_ref[...], high, preferred_element_type=jnp.float32) + jnp.dot(
@@ -230,8 +270,13 @@
         )
         mixed_ref[:, cols] = (weight_ref[...] * token_out).astype(jnp.bfloat16)
         wgrad_ref[...] += jnp.sum(dout_ref[:, cols].astype(jnp.float32) * token_out, axis=1, keepdims=True)
-        for off in range(1, n_sp):
-            r_send(step, off).wait_send()
+        if relayed:
+            for kind in range(3):
+                for way in range(2):
+                    r_hop(step, way, kind).wait_send()
+        else:
+            for off in range(1, n_sp):
+                r_send(step, off).wait_send()
         return carry
 
     lax.fori_loop(0, n_col, mix_step, 0)
@@ -310,8 +355,8 @@
             dma((n_sp,)),
             dma((n_sp,)),
             dma((n_sp,)),
-            dma((n_col, n_sp)),
-            dma((n_col, n_sp)),
+            dma((n_col, max(n_sp, 6))),
+            dma((n_col, max(n_sp, 6))),
             dma((4,)),
             dma((4,)),
         ],

time: 129 us -> 130 us (level)
  no operation moved by 1% of the time
where the time goes in v3:
time: 130 us; the launch traced here: 129 us
  Pallas kernels  101 us (78%)
  matrix products  13.9 us (11%)
  other arithmetic  10.6 us (8%)
  local copies, waits for them, and re-layouts  2.67 us (2%)
    pallas_call x1, Pallas kernels, exchange(): pl.pallas_call(functools.partial(exchange_kernel, n_dp, n_sp), out_shape=...  101 us
    dot_general x2, matrix products, contract_rows(): lax.dot_general(left, right, (((0,), (0,)), ((), ())), preferred_element_...  13.9 us
    convert_element_type x1, other arithmetic, local(): up_grads = (d_hidden * silu_gate).astype(jnp.bfloat16)  4.12 us

profile of v3, /device:TPU:0, one launch (start us, length us, event | category | flops | bytes accessed | tf_op | source)
XLA Modules:
  0.0 129.2 jit_solution(16198159486199275649)
XLA Ops:
  0.6 0.0 copy-start
  0.7 0.8 compare_reduce_fusion
  1.5 0.7 slice_compare_fusion
  2.2 0.8 fusion.16
  2.9 0.1 copy.46
  3.1 0.1 copy.52
  3.2 0.1 copy.47
  3.3 0.1 copy.45
  3.4 0.2 reduce-window.8
  3.6 0.1 add_reduce_fusion
  3.7 0.7 fusion.10.choose_ref
  4.5 0.1 copy.48
  4.6 0.7 fusion.15
  5.2 0.1 select_reduce_fusion
  5.4 2.8 %fusion.dslot_ref = bf16[64,6144]{1,0:T(8,128)(2,1)} fusion(bf16[128,6144]{1,0:T(8,128)(2,1)} %dout_ref.1, f32[64]{0:T(128)S(1)} %select_reduce_fusion, s32[128]{0:T(128)S(1)} %add_reduce_fusion, pred[128]{0:T(512)(128)(4,1)S(1)} %compare_reduce_fusion), kind=kOutput, calls=%fused_computation.1 | convolution fusion | flops 101466112 | bytes 2360192 | tf_op jit(solution)/shard_map/dot_general | solution.py:370
  8.2 1.7 %fusion.1.hid_ref = bf16[256,2048]{1,0:T(8,128)(2,1)} fusion(bf16[256,2048]{1,0:T(8,128)(2,1)S(1)} %copy-done, bf16[256,2048]{1,0:T(8,128)(2,1)S(1)} %copy-done.1), kind=kLoop, calls=%fused_computation.7 | loop fusion | flops 4194304 | bytes 3145728 | tf_op jit(solution)/shard_map/convert_element_type | solution.py:386
  9.8 101.3 %shard_map.101 = (f32[256,2048]{1,0:T(8,128)}, bf16[8,256,2048]{2,1,0:T(8,128)(2,1)}, bf16[8,4,64,768]{3,2,1,0:T(8,128)(2,1)}, bf16[128,6144]{1,0:T(8,128)(2,1)}, f32[128,1]{1,0:T(8,128)}) custom-call(bf16[256,2048]{1,0:T(8,128)(2,1)} %fusion.1.hid_ref, bf16[64,6144]{1,0:T(8,128)(2,1)} %fusion.dslot_ref, bf16[2048,6144]{1,0:T(8,128)(2,1)} %w_ref.1, ...), custom_call_target="tpu_custom_call" | custom-call | tf_op jit(solution)/shard_map/pallas_call | solution.py:329
  111.2 0.9 fusion.14
  112.0 0.1 copy.55
  112.1 0.1 copy.54
  112.2 0.6 pad_maximum_fusion
  112.8 4.1 %multiply_convert_fusion = (bf16[256,2048]{1,0:T(8,128)(2,1)}, bf16[256,2048]{1,0:T(8,128)(2,1)}) fusion(f32[256,2048]{1,0:T(8,128)} %get-tuple-element.12, bf16[256,2048]{1,0:T(8,128)(2,1)S(1)} %copy-done.1, bf16[256,2048]{1,0:T(8,128)(2,1)S(1)} %copy-done), kind=kLoop, calls=%fused_computation.15 | loop fusion | flops 7864320 | bytes 6291456 | tf_op jit(solution)/shard_map/convert_element_type | solution.py:409
  116.9 11.1 %fusion.17 = f32[2048,768]{1,0:T(8,128)} fusion(bf16[2048,2048]{1,0:T(8,128)(2,1)} %bitcast.8, bf16[2048,768]{1,0:T(8,128)(2,1)S(1)} %bitcast.9), kind=kOutput, calls=%fused_computation.32 | convolution fusion | flops 6442450944 | bytes 17825792 | tf_op jit(solution)/shard_map/dot_general | solution.py:370
  128.0 1.1 copy.57
  (10 shorter events, 0.0 us)
Async XLA Ops:
  0.6 7.5 %copy-start = (bf16[256,2048]{1,0:T(8,128)(2,1)S(1)}, bf16[256,2048]{1,0:T(8,128)(2,1)}, u32[]{:S(2)}) copy-start(bf16[256,2048]{1,0:T(8,128)(2,1)} %param.7) | copy-start | bytes 3145732
  0.6 7.5 %copy-start.1 = (bf16[256,2048]{1,0:T(8,128)(2,1)S(1)}, bf16[256,2048]{1,0:T(8,128)(2,1)}, u32[]{:S(2)}) copy-start(bf16[256,2048]{1,0:T(8,128)(2,1)} %param.6) | copy-start | bytes 3145732
  9.8 101.4 %copy-start.3 = (f32[128,1]{1,0:T(8,128)S(1)}, f32[128,1]{1,0:T(8,128)}, u32[]{:S(2)}) copy-start(f32[128,1]{1,0:T(8,128)} %get-tuple-element.28.weight_ref) | copy-start | bytes 1540
  112.8 4.1 %copy-start.4 = (bf16[8,4,64,768]{3,2,1,0:T(8,128)(2,1)S(1)}, bf16[8,4,64,768]{3,2,1,0:T(8,128)(2,1)}, u32[]{:S(2)}) copy-start(bf16[8,4,64,768]{3,2,1,0:T(8,128)(2,1)} %get-tuple-element.14) | copy-start | bytes 9437188
  116.9 11.1 %copy-start.2 = (bf16[128,6144]{1,0:T(8,128)(2,1)S(1)}, bf16[128,6144]{1,0:T(8,128)(2,1)}, u32[]{:S(2)}) copy-start(bf16[128,6144]{1,0:T(8,128)(2,1)} %get-tuple-element.38) | copy-start | bytes 4718596

commit v4 on v3

--- a/solution.py
+++ b/solution.py
@@ -62,30 +62,43 @@
         other = lax.rem(dp + off, n_dp)
         pltpu.make_async_copy(dall_ref.at[other, sp], dall_ref.at[other, sp], arecv.at[other]).wait()
 
+    half_slots = hid_ref.shape[0] // 2
+
+    def h_part(index, half):
+        return hall_ref.at[index, half * half_slots:(half + 1) * half_slots]
+
+    def own_part(half):
+        return hid_ref.at[half * half_slots:(half + 1) * half_slots]
+
+    def h_send(index, half, src, to, send):
+        return remote(src, h_part(index, half), send, hrecv.at[2 * index + half], dp=to)
+
+    def h_wait(index, half):
+        pltpu.make_async_copy(h_part(index, half), h_part(index, half), hrecv.at[2 * index + half]).wait()
+
+    def h_right(index, half, src, step):
+        return h_send(index, half, src, dp + 2, right_send.at[2 * step + half])
+
+    def h_left(index, half, src, step):
+        return h_send(index, half, src, dp - 2, left_send.at[2 * step + half])
+
+    def h_pair(index, half, src):
+        return h_send(index, half, src, chip * 2 + 1 - core, pair_send.at[2 * lax.div(index, 2) + half])
+
+    for half in range(2):
+        @pl.when(chip + 1 < chips)
+        def _():
+            h_right(dp, half, own_part(half), 0).start()
+
+        @pl.when(chip >= 1)
+        def _():
+            h_left(dp, half, own_part(half), 0).start()
+
+    for half in range(2):
+        h_pair(dp, half, own_part(half)).start()
+
     for off in range(1, n_dp):
         a_send(off).start()
-
-    def h_block(index, src=None):
-        return hall_ref.at[index]
-
-    def h_send(index, src, to_chip, send):
-        return remote(src, hall_ref.at[index], send, hrecv.at[index], dp=to_chip * 2 + core)
-
-    def h_pair(index, src, send):
-        return remote(src, hall_ref.at[index], send, hrecv.at[index], dp=chip * 2 + 1 - core)
-
-    def h_wait(index):
-        pltpu.make_async_copy(hall_ref.at[index], hall_ref.at[index], hrecv.at[index]).wait()
-
-    @pl.when(chip + 1 < chips)
-    def _():
-        h_send(dp, hid_ref, chip + 1, right_send.at[0]).start()
-
-    @pl.when(chip >= 1)
-    def _():
-        h_send(dp, hid_ref, chip - 1, left_send.at[0]).start()
-
-    h_pair(dp, hid_ref, pair_send.at[chip]).start()
 
     relayed = n_sp == 4
     if relayed:
@@ -185,10 +198,41 @@
         return carry
 
     lax.fori_loop(0, n_col, col_step, 0)
+
+    def relay(step, half):
+        @pl.when(chip - step >= 0)
+        def _():
+            index = dp - 2 * step
+            h_wait(index, half)
+
+            @pl.when(chip + 1 < chips)
+            def _():
+                h_right(index, half, h_part(index, half), step).start()
+
+            h_pair(index, half, h_part(index, half)).start()
+
+        @pl.when(chip + step < chips)
+        def _():
+            index = dp + 2 * step
+            h_wait(index, half)
+
+            @pl.when(chip >= 1)
+            def _():
+                h_left(index, half, h_part(index, half), step).start()
+
+            h_pair(index, half, h_part(index, half)).start()
+
     for way in ways:
         arrived(dcyc.at[near[way]], grecv.at[near[way]])
         if relayed:
             g_pass(way).start()
+
+    if chips > 1:
+        for half in range(2):
+            relay(1, half)
+
+    if relayed:
+        lax.fori_loop(0, n_col, fold_step, 0)
 
     for copy in own:
         copy.wait()
@@ -198,34 +242,7 @@
     for way in ways:
         b_send(way).start()
 
-    def relay(step):
-        @pl.when(chip - step >= 0)
-        def _():
-            index = (chip - step) * 2 + core
-            h_wait(index)
-
-            @pl.when(chip + 1 < chips)
-            def _():
-                h_send(index, h_block(index), chip + 1, right_send.at[step]).start()
-
-            h_pair(index, h_block(index), pair_send.at[chip - step]).start()
-
-        @pl.when(chip + step < chips)
-        def _():
-            index = (chip + step) * 2 + core
-            h_wait(index)
-
-            @pl.when(chip >= 1)
-            def _():
-                h_send(index, h_block(index), chip - 1, left_send.at[step]).start()
-
-            h_pair(index, h_block(index), pair_send.at[chip + step]).start()
-
-    for step in range(1, min(2, chips)):
-        relay(step)
-
     if relayed:
-        lax.fori_loop(0, n_col, fold_step, 0)
         for way in ways:
             arrived(g_half(3 - sp, way), frecv.at[way])
 
@@ -243,10 +260,10 @@
         )
         return carry
 
-    lax.fori_loop(0, n_row, row_step, 0)
-
-    for step in range(2, min(3, chips)):
-        relay(step)
+    for half in range(2):
+        lax.fori_loop(half * n_row // 2, (half + 1) * n_row // 2, row_step, 0)
+        if chips > 2:
+            relay(2, half)
 
     wgrad_ref[...] = jnp.zeros_like(wgrad_ref)
 
@@ -287,10 +304,12 @@
             b_pass(way).start()
 
     for step in range(3, chips):
-        relay(step)
+        for half in range(2):
+            relay(step, half)
 
     for index in range(chips):
-        h_wait(index * 2 + 1 - core)
+        for half in range(2):
+            h_wait(index * 2 + 1 - core, half)
     for way in ways:
         g_send(way).wait_send()
         b_send(way).wait_send()
@@ -301,18 +320,16 @@
     for off in range(1, n_dp):
         a_send(off).wait_send()
     for step in range(chips):
-
-        @pl.when((chip - step >= 0) & (chip + 1 < chips))
-        def _():
-            index = (chip - step) * 2 + core
-            h_send(index, hid_ref if step == 0 else h_block(index), chip + 1, right_send.at[step]).wait_send()
-
-        @pl.when((chip + step < chips) & (chip >= 1))
-        def _():
-            index = (chip + step) * 2 + core
-            h_send(index, hid_ref if step == 0 else h_block(index), chip - 1, left_send.at[step]).wait_send()
-
-        h_pair(dp, hid_ref, pair_send.at[step]).wait_send()
+        for half in range(2):
+            @pl.when((chip - step >= 0) & (chip + 1 < chips))
+            def _():
+                h_right(dp - 2 * step, half, own_part(half), step).wait_send()
+
+            @pl.when((chip + step < chips) & (chip >= 1))
+            def _():
+                h_left(dp + 2 * step, half, own_part(half), step).wait_send()
+
+            h_send(dp, half, own_part(half), chip * 2 + 1 - core, pair_send.at[2 * step + half]).wait_send()
 
 
 def exchange(n_dp, n_sp, hidden, d_slot, w_down, choose, weight, d_out):
@@ -345,10 +362,10 @@
             pltpu.VMEM((2, th, width), bf),
             dma((4,)),
             dma((4,)),
-            dma((chips,)),
-            dma((chips,)),
-            dma((chips,)),
-            dma((n_dp,)),
+            dma((2 * chips,)),
+            dma((2 * chips,)),
+            dma((2 * chips,)),
+            dma((2 * n_dp,)),
             dma((n_dp,)),
             dma((n_dp,)),
             dma((n_sp,)),

time: 130 us -> 123 us (0.946)
  Pallas kernels: 101 us -> 94.2 us
    pallas_call x1, Pallas kernels: 101 us -> 94.2 us  [exchange(): pl.pallas_call(functools.partial(exchange_kernel, n_dp, n_sp), out_shape=...]
where the time goes in v4:
time: 123 us; the launch traced here: 122 us
  Pallas kernels  94.2 us (77%)
  matrix products  13.9 us (11%)
  other arithmetic  10.6 us (9%)
  local copies, waits for them, and re-layouts  2.67 us (2%)
    pallas_call x1, Pallas kernels, exchange(): pl.pallas_call(functools.partial(exchange_kernel, n_dp, n_sp), out_shape=...  94.2 us
    dot_general x2, matrix products, contract_rows(): lax.dot_general(left, right, (((0,), (0,)), ((), ())), preferred_element_...  13.9 us
    convert_element_type x1, other arithmetic, local(): up_grads = (d_hidden * silu_gate).astype(jnp.bfloat16)  4.12 us

profile of v4, /device:TPU:0, one launch (start us, length us, event | category | flops | bytes accessed | tf_op | source)
XLA Modules:
  0.0 122.0 jit_solution(8777386269040685990)
XLA Ops:
  0.7 0.8 compare_reduce_fusion
  1.5 0.7 slice_compare_fusion
  2.2 0.8 fusion.16
  2.9 0.1 copy.46
  3.1 0.1 copy.52
  3.2 0.1 copy.47
  3.3 0.1 copy.45
  3.4 0.2 reduce-window.8
  3.6 0.1 add_reduce_fusion
  3.7 0.7 fusion.10.choose_ref
  4.5 0.1 copy.48
  4.6 0.7 fusion.15
  5.2 0.1 select_reduce_fusion
  5.4 2.8 %fusion.dslot_ref = bf16[64,6144]{1,0:T(8,128)(2,1)} fusion(bf16[128,6144]{1,0:T(8,128)(2,1)} %dout_ref.1, f32[64]{0:T(128)S(1)} %select_reduce_fusion, s32[128]{0:T(128)S(1)} %add_reduce_fusion, pred[128]{0:T(512)(128)(4,1)S(1)} %compare_reduce_fusion), kind=kOutput, calls=%fused_computation.1 | convolution fusion | flops 101466112 | bytes 2360192 | tf_op jit(solution)/shard_map/dot_general | solution.py:387
  8.2 0.0 copy-done
  8.2 1.7 %fusion.1.hid_ref = bf16[256,2048]{1,0:T(8,128)(2,1)} fusion(bf16[256,2048]{1,0:T(8,128)(2,1)S(1)} %copy-done, bf16[256,2048]{1,0:T(8,128)(2,1)S(1)} %copy-done.1), kind=kLoop, calls=%fused_computation.7 | loop fusion | flops 4194304 | bytes 3145728 | tf_op jit(solution)/shard_map/convert_element_type | solution.py:403
  9.8 94.2 %shard_map.101 = (f32[256,2048]{1,0:T(8,128)}, bf16[8,256,2048]{2,1,0:T(8,128)(2,1)}, bf16[8,4,64,768]{3,2,1,0:T(8,128)(2,1)}, bf16[128,6144]{1,0:T(8,128)(2,1)}, f32[128,1]{1,0:T(8,128)}) custom-call(bf16[256,2048]{1,0:T(8,128)(2,1)} %fusion.1.hid_ref, bf16[64,6144]{1,0:T(8,128)(2,1)} %fusion.dslot_ref, bf16[2048,6144]{1,0:T(8,128)(2,1)} %w_ref.1, ...), custom_call_target="tpu_custom_call" | custom-call | tf_op jit(solution)/shard_map/pallas_call | solution.py:346
  104.1 0.9 fusion.14
  104.9 0.1 copy.55
  105.0 0.1 copy.54
  105.1 0.6 pad_maximum_fusion
  105.7 4.1 %multiply_convert_fusion = (bf16[256,2048]{1,0:T(8,128)(2,1)}, bf16[256,2048]{1,0:T(8,128)(2,1)}) fusion(f32[256,2048]{1,0:T(8,128)} %get-tuple-element.12, bf16[256,2048]{1,0:T(8,128)(2,1)S(1)} %copy-done.1, bf16[256,2048]{1,0:T(8,128)(2,1)S(1)} %copy-done), kind=kLoop, calls=%fused_computation.15 | loop fusion | flops 7864320 | bytes 6291456 | tf_op jit(solution)/shard_map/convert_element_type | solution.py:426
  109.8 11.1 %fusion.17 = f32[2048,768]{1,0:T(8,128)} fusion(bf16[2048,2048]{1,0:T(8,128)(2,1)} %bitcast.8, bf16[2048,768]{1,0:T(8,128)(2,1)S(1)} %bitcast.9), kind=kOutput, calls=%fused_computation.32 | convolution fusion | flops 6442450944 | bytes 17825792 | tf_op jit(solution)/shard_map/dot_general | solution.py:387
  120.9 1.1 copy.57
  (10 shorter events, 0.0 us)
Async XLA Ops:
  0.6 7.5 %copy-start = (bf16[256,2048]{1,0:T(8,128)(2,1)S(1)}, bf16[256,2048]{1,0:T(8,128)(2,1)}, u32[]{:S(2)}) copy-start(bf16[256,2048]{1,0:T(8,128)(2,1)} %param.7) | copy-start | bytes 3145732
  0.6 7.5 %copy-start.1 = (bf16[256,2048]{1,0:T(8,128)(2,1)S(1)}, bf16[256,2048]{1,0:T(8,128)(2,1)}, u32[]{:S(2)}) copy-start(bf16[256,2048]{1,0:T(8,128)(2,1)} %param.6) | copy-start | bytes 3145732
  9.8 94.2 %copy-start.3 = (f32[128,1]{1,0:T(8,128)S(1)}, f32[128,1]{1,0:T(8,128)}, u32[]{:S(2)}) copy-start(f32[128,1]{1,0:T(8,128)} %get-tuple-element.28.weight_ref) | copy-start | bytes 1540
  105.7 4.1 %copy-start.4 = (bf16[8,4,64,768]{3,2,1,0:T(8,128)(2,1)S(1)}, bf16[8,4,64,768]{3,2,1,0:T(8,128)(2,1)}, u32[]{:S(2)}) copy-start(bf16[8,4,64,768]{3,2,1,0:T(8,128)(2,1)} %get-tuple-element.14) | copy-start | bytes 9437188
  109.8 11.1 %copy-start.2 = (bf16[128,6144]{1,0:T(8,128)(2,1)S(1)}, bf16[128,6144]{1,0:T(8,128)(2,1)}, u32[]{:S(2)}) copy-start(bf16[128,6144]{1,0:T(8,128)(2,1)} %get-tuple-element.38) | copy-start | bytes 4718596

commit v5 on v4

--- a/solution.py
+++ b/solution.py
@@ -11,9 +11,9 @@
 
 
 def exchange_kernel(
-    n_dp, n_sp, hid_ref, dslot_ref, w_ref, choose_ref, weight_ref, dout_ref,
+    n_dp, n_sp, hid_ref, slot_choose_ref, slot_weight_ref, w_ref, choose_ref, weight_ref, dout_ref,
     dhid_ref, hall_ref, dall_ref, mixed_ref, wgrad_ref,
-    part, rs_ref, dcyc, wcol, wrow, wsem, local_sem,
+    dslot_ref, part, rs_ref, dcyc, wcol, wrow, wsem, local_sem,
     right_send, left_send, pair_send, hrecv, asend, arecv, gsend, grecv, bsend, brecv, rsend, rrecv, fsend, frecv,
 ):
     dp, sp = lax.axis_index("dp"), lax.axis_index("sp")
@@ -96,6 +96,14 @@
 
     for half in range(2):
         h_pair(dp, half, own_part(half)).start()
+
+    def slot_step(step, carry):
+        cols = pl.ds(pl.multiple_of(step * tn, tn), tn)
+        picked = jnp.dot(slot_choose_ref[...], dout_ref[:, cols], preferred_element_type=jnp.float32)
+        dslot_ref[:, cols] = (slot_weight_ref[...] * picked).astype(jnp.bfloat16)
+        return carry
+
+    lax.fori_loop(0, n_col, slot_step, 0)
 
     for off in range(1, n_dp):
         a_send(off).start()
@@ -332,9 +340,9 @@
             h_send(dp, half, own_part(half), chip * 2 + 1 - core, pair_send.at[2 * step + half]).wait_send()
 
 
-def exchange(n_dp, n_sp, hidden, d_slot, w_down, choose, weight, d_out):
+def exchange(n_dp, n_sp, hidden, slot_choose, slot_weight, w_down, choose, weight, d_out):
     slots, hid_width = hidden.shape
-    slot_rows, width = d_slot.shape
+    slot_rows, width = slot_choose.shape[0], d_out.shape[1]
     block = width // n_dp
     tn, th = width // 8, min(256, hid_width)
     n_col = width // tn
@@ -352,9 +360,10 @@
             jax.ShapeDtypeStruct(d_out.shape, bf),
             jax.ShapeDtypeStruct((d_out.shape[0], 1), jnp.float32),
         ),
-        in_specs=[vmem, vmem, hbm, vmem, vmem, vmem],
+        in_specs=[vmem, vmem, vmem, hbm, vmem, vmem, vmem],
         out_specs=(vmem, hbm, hbm, vmem, vmem),
         scratch_shapes=[
+            pltpu.VMEM((slot_rows, width), bf),
             pltpu.VMEM((n_sp, slot_rows, width), bf),
             pltpu.VMEM((n_sp, slot_rows, width), bf),
             pltpu.VMEM((n_sp, slot_rows, width), bf),
@@ -380,7 +389,7 @@
         compiler_params=pltpu.CompilerParams(
             collective_id=0, has_side_effects=True, vmem_limit_bytes=60 * 1024 * 1024
         ),
-    )(hidden, d_slot, w_down, choose, weight, d_out)
+    )(hidden, slot_choose, slot_weight, w_down, choose, weight, d_out)
 
 
 def contract_rows(left, right):
@@ -408,11 +417,9 @@
     chooser = (slot_rank[:, None] == jnp.arange(slot_rows, dtype=jnp.int32)[None, :]) & routed[
         :, None
     ]
-    picked = contract_rows(chooser.astype(jnp.bfloat16), d_out)
     slot_weight = jnp.sum(jnp.where(chooser, weight_zero[:, None], 0.0), axis=0)
-    d_slot = (slot_weight[:, None] * picked).astype(jnp.bfloat16)
     d_hidden, hidden_all, d_all, mixed, weight_grad = exchange(
-        n_dp, n_sp, hidden, d_slot, w_down, chooser.astype(jnp.bfloat16), weight_zero[:, None], d_out
+        n_dp, n_sp, hidden, chooser.T.astype(jnp.bfloat16), slot_weight[:, None], w_down, chooser.astype(jnp.bfloat16), weight_zero[:, None], d_out
     )
     logit_grad = weight_grad[:, 0] * weight_zero * (1.0 - weight_zero)
     first_col = jnp.where(first_zero, logit_grad, -logit_grad)

time: 123 us -> 122 us (level)
  matrix products: 13.9 us -> 11.1 us
  other arithmetic: 10.6 us -> 12.6 us
    dot_general x2 -> x1, matrix products: 13.9 us -> 11.1 us  [contract_rows(): lax.dot_general(left, right, (((0,), (0,)), ((), ())), preferred_element_...]
    convert_element_type x1, other arithmetic: 1.66 us -> 3.18 us  [local(): hidden = (silu_gate * up_wide).astype(jnp.bfloat16)]
where the time goes in v5:
time: 122 us
  Pallas kernels  94.1 us (77%)
  other arithmetic  12.6 us (10%)
  matrix products  11.1 us (9%)
  local copies, waits for them, and re-layouts  3.38 us (3%)
    pallas_call x1, Pallas kernels, exchange(): pl.pallas_call(functools.partial(exchange_kernel, n_dp, n_sp), out_shape=...  94.1 us
    dot_general x1, matrix products, contract_rows(): lax.dot_general(left, right, (((0,), (0,)), ((), ())), preferred_element_...  11.1 us
    convert_element_type x1, other arithmetic, local(): up_grads = (d_hidden * silu_gate).astype(jnp.bfloat16)  4.12 us
    convert_element_type x1, other arithmetic, local(): hidden = (silu_gate * up_wide).astype(jnp.bfloat16)  3.18 us

profile of v5, /device:TPU:0, one launch (start us, length us, event | category | flops | bytes accessed | tf_op | source)
XLA Modules:
  0.0 121.9 jit_solution(460134272127837866)
XLA Ops:
  0.6 0.7 compare_reduce_fusion
  1.3 0.7 slice_compare_fusion
  2.0 0.8 fusion.14
  2.8 0.1 copy.49
  2.9 0.1 copy.55
  3.1 0.1 copy.50
  3.2 0.1 copy.48
  3.3 0.2 reduce-window.8
  3.5 0.1 add_reduce_fusion
  3.6 0.6 fusion.11.slot_choose_ref
  4.2 0.7 fusion.9.choose_ref
  4.9 0.1 copy.51
  5.0 0.7 fusion.13
  5.7 0.1 select_reduce_fusion
  5.8 0.7 copy.56.slot_weight_ref
  6.5 3.2 %fusion.hid_ref = bf16[256,2048]{1,0:T(8,128)(2,1)} fusion(bf16[256,2048]{1,0:T(8,128)(2,1)} %param.7, bf16[256,2048]{1,0:T(8,128)(2,1)} %param.6), kind=kLoop, calls=%fused_computation.5 | loop fusion | flops 4194304 | bytes 3145728 | tf_op jit(solution)/shard_map/convert_element_type | solution.py:412
  9.7 94.1 %shard_map.101 = (f32[256,2048]{1,0:T(8,128)}, bf16[8,256,2048]{2,1,0:T(8,128)(2,1)}, bf16[8,4,64,768]{3,2,1,0:T(8,128)(2,1)}, bf16[128,6144]{1,0:T(8,128)(2,1)}, f32[128,1]{1,0:T(8,128)}) custom-call(bf16[256,2048]{1,0:T(8,128)(2,1)} %fusion.hid_ref, bf16[64,128]{1,0:T(8,128)(2,1)} %fusion.11.slot_choose_ref, f32[64,1]{1,0:T(8,128)} %copy.56.slot_weight_ref, ...), custom_call_target="tpu_custom_call" | custom-call | tf_op jit(solution)/shard_map/pallas_call | solution.py:354
  103.9 0.9 fusion.12
  104.7 0.1 copy.59
  104.8 0.1 copy.58
  104.9 0.6 pad_maximum_fusion
  105.5 4.1 %multiply_convert_fusion = (bf16[256,2048]{1,0:T(8,128)(2,1)}, bf16[256,2048]{1,0:T(8,128)(2,1)}) fusion(f32[256,2048]{1,0:T(8,128)} %get-tuple-element.12, bf16[256,2048]{1,0:T(8,128)(2,1)S(1)} %copy-done.1, bf16[256,2048]{1,0:T(8,128)(2,1)S(1)} %copy-done), kind=kLoop, calls=%fused_computation.13 | loop fusion | flops 7864320 | bytes 6291456 | tf_op jit(solution)/shard_map/convert_element_type | solution.py:433
  109.6 11.1 %fusion.15 = f32[2048,768]{1,0:T(8,128)} fusion(bf16[2048,2048]{1,0:T(8,128)(2,1)} %bitcast.9, bf16[2048,768]{1,0:T(8,128)(2,1)S(1)} %bitcast.10), kind=kOutput, calls=%fused_computation.31 | convolution fusion | flops 6442450944 | bytes 17825792 | tf_op jit(solution)/shard_map/dot_general | solution.py:396
  120.7 1.1 copy.61
  (11 shorter events, 0.0 us)
Async XLA Ops:
  9.7 94.2 %copy-start.3 = (f32[128,1]{1,0:T(8,128)S(1)}, f32[128,1]{1,0:T(8,128)}, u32[]{:S(2)}) copy-start(f32[128,1]{1,0:T(8,128)} %get-tuple-element.28.weight_ref) | copy-start | bytes 1540
  9.7 95.8 %copy-start = (bf16[256,2048]{1,0:T(8,128)(2,1)S(1)}, bf16[256,2048]{1,0:T(8,128)(2,1)}, u32[]{:S(2)}) copy-start(bf16[256,2048]{1,0:T(8,128)(2,1)} %param.7) | copy-start | bytes 3145732
  9.7 95.8 %copy-start.1 = (bf16[256,2048]{1,0:T(8,128)(2,1)S(1)}, bf16[256,2048]{1,0:T(8,128)(2,1)}, u32[]{:S(2)}) copy-start(bf16[256,2048]{1,0:T(8,128)(2,1)} %param.6) | copy-start | bytes 3145732
  105.5 4.1 %copy-start.4 = (bf16[8,4,64,768]{3,2,1,0:T(8,128)(2,1)S(1)}, bf16[8,4,64,768]{3,2,1,0:T(8,128)(2,1)}, u32[]{:S(2)}) copy-start(bf16[8,4,64,768]{3,2,1,0:T(8,128)(2,1)} %get-tuple-element.14) | copy-start | bytes 9437188
  109.6 11.1 %copy-start.2 = (bf16[128,6144]{1,0:T(8,128)(2,1)S(1)}, bf16[128,6144]{1,0:T(8,128)(2,1)}, u32[]{:S(2)}) copy-start(bf16[128,6144]{1,0:T(8,128)(2,1)} %get-tuple-element.38) | copy-start | bytes 4718596
